TPU v7x, 32 devices: a whole 2x2x4 slice. The times are simulated.
32 devices in a mesh: dp: 2 (over y), fsdp: 16 (over z, x, core).
Axes of the slice: x: 2, y: 2, z: 4, core: 2. Of those that a mesh axis runs over, the one named last changes fastest.
Arguments:
- ids: int32 [2, 192], P('dp'), may hold values from 0 to 511
- embed: bfloat16 [512, 8192], P(None, 'fsdp'), may hold values from -32 to 32
- gain: bfloat16 [8192], P('fsdp'), may hold values from 0.099609375 to 1.8984375
- w_in: bfloat16 [3, 4096, 8192], P(None, 'fsdp'), may hold values from -0.0625 to 0.0625
- feat_filter: float32 [3, 256, 7], P(None, 'fsdp'), may hold values from -2.4 to 2.4
- inner_filter: float32 [256, 7], P('fsdp'), may hold values from -2.4 to 2.4
- w_out: bfloat16 [4096, 8192], P(None, 'fsdp'), may hold values from -0.09375 to 0.09375
- cotangent: bfloat16 [2, 192, 8192], P('dp', None, 'fsdp'), may hold values from -6 to 6
- right_prev: bfloat16 [8192, 256], P('fsdp'), may hold values from -6 to 6
Outputs:
- block_out: bfloat16 [2, 192, 8192], P('dp', None, 'fsdp')
- filter_grad: float32 [4, 256, 7], P(None, 'fsdp')
- basis: bfloat16 [4096, 256], P('fsdp')
- right_factor: float32 [8192, 256], P('fsdp')
All inputs are finite; a program needn't handle non-finite values.
Results may differ from a plain program's by a relative error of at most 0.014.
The roundings to bfloat16 on the way count: a program that leaves them out, or rounds other values in their place, can miss the bound.
Values may be sent and summed in bfloat16 or wider, within the bound.
No kernel may reach another device: no remote copies, remote signals or barrier semaphores. Data moves between devices by JAX's collectives and lax.ppermute only.
A program may use at most 128 MiB of HBM per device.

v0:
```python
import jax
import jax.numpy as jnp
from jax import lax
from jax.sharding import PartitionSpec as P

D = 8192
C = 4096
GROUP = 16


def shifted(signal, lag, tap_count):
    padded = jnp.pad(signal, ((tap_count - 1, 0), (0, 0)))
    first = tap_count - 1 - lag
    return padded[first : first + signal.shape[0]]


def causal(signal, tap_table):
    tap_count = tap_table.shape[0]
    result = jnp.zeros(signal.shape, jnp.float32)
    for lag in range(tap_count):
        result = result + tap_table[lag][None, :] * shifted(signal, lag, tap_count)
    return result


def anticausal(signal, tap_table):
    tap_count = tap_table.shape[0]
    padded = jnp.pad(signal, ((0, tap_count - 1), (0, 0)))
    result = jnp.zeros(signal.shape, jnp.float32)
    for lag in range(tap_count):
        result = result + tap_table[lag][None, :] * padded[lag : lag + signal.shape[0]]
    return result


def tap_sums(gradient, signal, tap_count):
    listing = []
    for lag in range(tap_count):
        listing.append(jnp.sum(gradient * shifted(signal, lag, tap_count), axis=0))
    stacked = jnp.stack(listing, axis=0)
    grouped = stacked.reshape(tap_count, stacked.shape[1] // GROUP, GROUP).sum(axis=2)
    return grouped.T


def expand(filters):
    return jnp.repeat(filters.T, GROUP, axis=1)


def per_device(ids, embed, gain, w_in, feat_filter, inner_filter, w_out, cotangent, right_prev):
    tokens = ids[0]
    length = tokens.shape[0]
    tap_count = inner_filter.shape[1]
    onehot = (tokens[:, None] == jnp.arange(embed.shape[0], dtype=jnp.int32)[None, :]).astype(
        jnp.bfloat16
    )
    x_cols = jnp.dot(onehot, embed, preferred_element_type=jnp.float32)
    square_sums = lax.psum(jnp.sum(x_cols * x_cols, axis=1), "fsdp")
    factor = lax.rsqrt(square_sums / D + 1e-05)
    normed_cols = (x_cols * factor[:, None] * gain.astype(jnp.float32)[None, :]).astype(
        jnp.bfloat16
    )
    projected = jnp.einsum(
        "ld,kcd->klc",
        lax.all_gather(normed_cols, "fsdp", axis=1, tiled=True),
        w_in,
        preferred_element_type=jnp.float32,
    )
    rounded = lax.optimization_barrier(projected.astype(jnp.bfloat16)).astype(jnp.float32)
    query, key_in, value = (rounded[0], rounded[1], rounded[2])
    query_conv = causal(query, expand(feat_filter[0]))
    key_conv = causal(key_in, expand(feat_filter[1]))
    value_conv = causal(value, expand(feat_filter[2]))
    gated = key_conv * value_conv
    inner_table = expand(inner_filter)
    window = causal(gated, inner_table)
    gated_out = (query_conv * window).astype(jnp.bfloat16)
    cot_cols = cotangent[0]
    shard_piece = lax.all_gather(gated_out, "fsdp", axis=1, tiled=True)
    weight_rows = w_out
    mixed_sum = jnp.dot(shard_piece, weight_rows, preferred_element_type=jnp.float32)
    term = jnp.einsum("lc,ld->cd", shard_piece, cot_cols, preferred_element_type=jnp.float32)
    mixed_sum, grad_part = (mixed_sum, term)
    block_out = (x_cols + mixed_sum).astype(jnp.bfloat16)[None]
    weight_rows = w_out
    mixed_grad = lax.psum_scatter(
        jnp.einsum("cd,ld->cl", weight_rows, cot_cols, preferred_element_type=jnp.float32),
        "fsdp",
        scatter_dimension=0,
        tiled=True,
    ).T
    query_grad = mixed_grad * window
    window_grad = mixed_grad * query_conv
    gated_grad = anticausal(window_grad, inner_table)
    key_grad = gated_grad * value_conv
    value_grad = gated_grad * key_conv
    norm_factor = 1.0 / jnp.sqrt(jnp.float32(lax.axis_size("dp") * length))
    filter_part = (
        jnp.stack(
            [
                tap_sums(query_grad, query, tap_count),
                tap_sums(key_grad, key_in, tap_count),
                tap_sums(value_grad, value, tap_count),
                tap_sums(window_grad, gated, tap_count),
            ],
            axis=0,
        )
        * norm_factor
    )
    grad_total, filter_grad = (
        lax.psum(grad_part.astype(jnp.bfloat16), "dp").astype(jnp.float32),
        lax.psum(filter_part.astype(jnp.bfloat16), "dp").astype(jnp.float32),
    )
    grad_half = grad_total.astype(jnp.bfloat16)
    grad_rows_own = lax.all_to_all(grad_half, "fsdp", split_axis=0, concat_axis=1, tiled=True)
    panel_own = jnp.dot(
        grad_rows_own,
        lax.all_gather(right_prev, "fsdp", axis=0, tiled=True),
        preferred_element_type=jnp.float32,
    ).astype(jnp.bfloat16)
    root_scale = jnp.sqrt(jnp.float32(C))
    gram_local = jnp.einsum("cr,cs->rs", panel_own, panel_own, preferred_element_type=jnp.float32)
    gram_matrix = lax.psum(gram_local, "fsdp")
    lower_factor = jnp.linalg.cholesky(gram_matrix)
    solved = jax.scipy.linalg.solve_triangular(
        lower_factor, panel_own.astype(jnp.float32).T, lower=True
    ).T
    basis_own = (solved * root_scale).astype(jnp.bfloat16)
    right_raw = jnp.einsum(
        "cd,cr->dr",
        grad_half,
        lax.all_gather(basis_own, "fsdp", axis=0, tiled=True),
        preferred_element_type=jnp.float32,
    )
    column_sums = lax.psum(jnp.sum(right_raw * right_raw, axis=0), "fsdp")
    right_factor = right_raw * lax.rsqrt(column_sums / D + 1e-06)[None, :]
    return (block_out, filter_grad, basis_own, right_factor)


def solution(mesh):
    placed = (
        P("dp", None),
        P(None, "fsdp"),
        P("fsdp"),
        P(None, "fsdp", None),
        P(None, "fsdp", None),
        P("fsdp", None),
        P(None, "fsdp"),
        P("dp", None, "fsdp"),
        P("fsdp", None),
    )
    return jax.shard_map(
        per_device,
        mesh=mesh,
        in_specs=placed,
        out_specs=(P("dp", None, "fsdp"), P(None, "fsdp", None), P("fsdp", None), P("fsdp", None)),
        check_vma=False,
    )
```

profile of v0, /device:TPU:0, one launch (start us, length us, event | category | flops | bytes accessed | tf_op | source)
XLA Modules:
  0.0 699.4 jit_solution(17935779332028869934)
XLA Ops:
  9.3 34.9 %psum.35 = f32[192]{0:T(256)S(1)} all-reduce(f32[192]{0:T(256)S(1)} %get-tuple-element.121), channel_id=1, replica_groups=mesh['dp'=2,'fsdp'=16] {'fsdp'}, use_global_device_ids=true, to_apply=%region_1.0 | all-reduce | flops 192 | bytes 1536 | tf_op jit(solution)/shard_map/psum | solution.py:55
  45.1 5.4 fusion.14
  55.0 34.7 %all-gather.5.cloned.1.call-done = bf16[192,8192]{1,0:T(8,128)(2,1)} async-done(((bf16[192,512]{1,0:T(8,128)(2,1)}), bf16[192,8192]{1,0:T(8,128)(2,1)}) %all-gather.5.cloned.1.call-update) | async-done | bytes 3145744 | tf_op jit(solution)/shard_map/all_gather | solution.py:62
  89.7 9.8 %fusion.6 = bf16[3,192,256]{2,1,0:T(8,128)(2,1)S(1)} fusion(bf16[3,256,8192]{2,1,0:T(8,128)(2,1)} %param.12, bf16[192,8192]{1,0:T(8,128)(2,1)} %all-gather.5.cloned.1.call-done), kind=kOutput, calls=%fused_computation.8 | convolution fusion | flops 2416066560 | bytes 16023552 | tf_op jit(solution)/shard_map/ld,kcd->klc/dot_general | solution.py:60
  99.6 58.3 %reduce-scatter.2.cloned.1.call-done = f32[256,192]{0,1:T(8,128)} async-done(((f32[4096,192]{0,1:T(8,128)}), f32[256,192]{0,1:T(8,128)}) %reduce-scatter.2.cloned.1.call-update) | async-done | bytes 196624 | tf_op jit(solution)/shard_map/reduce_scatter | solution.py:83
  161.0 2.6 multiply_reduce_fusion.23
  164.3 38.0 %all-gather.7.cloned.1.call-done = bf16[192,4096]{1,0:T(8,128)(2,1)} async-done(((bf16[192,256]{1,0:T(8,128)(2,1)}), bf16[192,4096]{1,0:T(8,128)(2,1)}) %all-gather.7.cloned.1.call-update) | async-done | bytes 1572880 | tf_op jit(solution)/shard_map/all_gather | solution.py:76
  202.3 4.7 convolution_convert_fusion
  207.7 106.5 %all-reduce.9.cloned.1.call-done = bf16[4096,512]{1,0:T(8,128)(2,1)} async-done(((bf16[4096,512]{1,0:T(8,128)(2,1)}), bf16[4096,512]{1,0:T(8,128)(2,1)}) %all-reduce.9.cloned.1.call-update) | async-done | bytes 4194320 | tf_op jit(solution)/shard_map/psum | solution.py:108
  314.2 6.4 copy.22
  320.6 5.7 all-to-all-start
  326.3 94.7 %all-gather.9.cloned.1.call-done = bf16[8192,256]{1,0:T(8,128)(2,1)} async-done(((bf16[512,256]{1,0:T(8,128)(2,1)}), bf16[8192,256]{1,0:T(8,128)(2,1)}) %all-gather.9.cloned.1.call-update) | async-done | bytes 4194320 | tf_op jit(solution)/shard_map/all_gather | solution.py:115
  421.0 6.5 all-to-all-done
  427.4 4.8 convolution_convert_fusion.1
  434.0 103.0 %all-reduce.11.cloned.1.call-done = f32[256,256]{0,1:T(8,128)} async-done(((f32[256,256]{0,1:T(8,128)}), f32[256,256]{0,1:T(8,128)}) %all-reduce.11.cloned.1.call-update) | async-done | bytes 262160 | tf_op jit(solution)/shard_map/psum | solution.py:120
  537.0 1.8 copy.24
  540.6 11.7 %cholesky.50 = f32[128,128]{1,0:T(8,128)S(1)} custom-call(f32[128,128]{1,0:T(8,128)S(1)} %cholesky.118), custom_call_target="Cholesky" | custom-call | tf_op jit(solution)/shard_map/jit(cholesky)/cholesky | solution.py:121
  553.6 9.8 %custom-call.15 = f32[1,128,128]{1,2,0:T(8,128)S(1)} custom-call(f32[1,128,128]{2,1,0:T(8,128)S(1)} %get-tuple-element.89), custom_call_target="InvertDiagBlocksLowerTriangular" | custom-call | tf_op jit(solution)/shard_map/jit(cholesky)/cholesky | solution.py:121
  563.4 1.7 constant_dynamic-update-slice_fusion.29
  566.2 11.7 %cholesky.105 = f32[128,128]{1,0:T(8,128)S(1)} custom-call(f32[128,128]{1,0:T(8,128)S(1)} %convolution_subtract_fusion.1), custom_call_target="Cholesky" | custom-call | tf_op jit(solution)/shard_map/jit(cholesky)/cholesky | solution.py:121
  581.7 1.7 select_select_fusion
  584.2 6.8 while.1
  584.8 2.9 bitcast_dynamic-update-slice_fusion.2
  588.2 2.8 bitcast_dynamic-update-slice_fusion.2
  591.0 20.5 %custom-call.16 = f32[2,128,128]{1,2,0:T(8,128)S(1)} custom-call(f32[2,128,128]{2,1,0:T(8,128)} %get-tuple-element.11), custom_call_target="InvertDiagBlocksLowerTriangular" | custom-call | tf_op jit(solution)/shard_map/jit(_solve_triangular)/triangular_solve | solution.py:122
  614.0 1.9 multiply_reduce_fusion.2
  616.6 2.0 multiply_reduce_fusion.29
  622.1 5.0 psum.36
  627.8 3.8 fusion.9
  632.4 23.5 %all-gather.11.cloned.1.call-done = bf16[4096,256]{0,1:T(8,128)(2,1)} async-done(((bf16[256,256]{0,1:T(8,128)(2,1)}), bf16[4096,256]{0,1:T(8,128)(2,1)}) %all-gather.11.cloned.1.call-update) | async-done | bytes 2097168 | tf_op jit(solution)/shard_map/all_gather | solution.py:129
  655.9 4.2 multiply_reduce_fusion
  660.1 31.6 %psum.39 = f32[256]{0:T(256)S(1)} all-reduce(f32[256]{0:T(256)S(1)} %get-tuple-element.125), channel_id=1, replica_groups=mesh['dp'=2,'fsdp'=16] {'fsdp'}, use_global_device_ids=true, to_apply=%region_43.44 | all-reduce | flops 256 | bytes 2048 | tf_op jit(solution)/shard_map/psum | solution.py:132
  (190 shorter events, 31.1 us)
Async XLA Ops:
  7.2 1.1 copy-start
  7.2 82.5 %all-gather.5.cloned.1.call-start = ((), (), s32[]{:S(2)}) async-start(), calls=%async_computation.2 | async-start | bytes 3342336 | tf_op jit(solution)/shard_map/all_gather | solution.py:62
  45.0 5.5 copy-start.8
  45.0 6.6 copy-start.9
  45.1 112.9 %reduce-scatter.2.cloned.1.call-start = ((), (), s32[]{:S(2)}) async-start(), calls=%async_computation.4 | async-start | bytes 3342336 | tf_op jit(solution)/shard_map/reduce_scatter | solution.py:83
  50.5 151.8 %all-gather.7.cloned.1.call-start = ((), (), s32[]{:S(2)}) async-start(), calls=%async_computation.3 | async-start | bytes 1671168 | tf_op jit(solution)/shard_map/all_gather | solution.py:76
  99.5 102.8 %copy-start.7 = (bf16[1,192,512]{2,1,0:T(8,128)(2,1)S(1)}, bf16[1,192,512]{2,1,0:T(8,128)(2,1)}, u32[]{:S(2)}) copy-start(bf16[1,192,512]{2,1,0:T(8,128)(2,1)} %param.16) | copy-start | bytes 589828
  99.6 61.3 %copy-start.3 = (f32[192,256]{1,0:T(8,128)}, f32[192,256]{1,0:T(8,128)S(1)}, u32[]{:S(2)}) copy-start(f32[192,256]{1,0:T(8,128)S(1)} %get-tuple-element.84) | copy-start | bytes 589828
  159.1 48.0 %copy-start.4 = (f32[192,256]{1,0:T(8,128)}, f32[192,256]{1,0:T(8,128)S(1)}, u32[]{:S(2)}) copy-start(f32[192,256]{1,0:T(8,128)S(1)} %get-tuple-element.79) | copy-start | bytes 589828
  161.0 46.1 %copy-start.2 = (f32[192,256]{1,0:T(8,128)}, f32[192,256]{1,0:T(8,128)S(1)}, u32[]{:S(2)}) copy-start(f32[192,256]{1,0:T(8,128)S(1)} %mul.459) | copy-start | bytes 589828
  164.2 150.0 %all-reduce.9.cloned.1.call-start = ((), (), s32[]{:S(2)}) async-start(), calls=%async_computation.5 | async-start | bytes 8388608 | tf_op jit(solution)/shard_map/psum | solution.py:108
  207.1 213.9 %all-gather.9.cloned.1.call-start = ((), (), s32[]{:S(2)}) async-start(), calls=%async_computation.6 | async-start | bytes 4456448 | tf_op jit(solution)/shard_map/all_gather | solution.py:115
  320.6 106.8 %all-to-all-start = ((bf16[16,256,512]{1,2,0:T(8,128)(2,1)}), bf16[16,256,512]{1,2,0:T(8,128)(2,1)}, u32[]{:S(2)}, u32[]{:S(2)}) async-start(bf16[16,256,512]{1,2,0:T(8,128)(2,1)} %copy.22), calls=%async_computation.1 | async-start | bytes 8388608 | tf_op jit(solution)/shard_map/all_to_all | solution.py:112
  326.2 210.8 %all-reduce.11.cloned.1.call-start = ((), (), s32[]{:S(2)}) async-start(), calls=%async_computation.7 | async-start | bytes 524288 | tf_op jit(solution)/shard_map/psum | solution.py:120
  433.2 222.7 %all-gather.11.cloned.1.call-start = ((), (), s32[]{:S(2)}) async-start(), calls=%async_computation.8 | async-start | bytes 2228224 | tf_op jit(solution)/shard_map/all_gather | solution.py:129
  434.0 193.8 %copy-start.1 = (bf16[192,4096]{1,0:T(8,128)(2,1)S(1)}, bf16[192,4096]{1,0:T(8,128)(2,1)}, u32[]{:S(2)}) copy-start(bf16[192,4096]{1,0:T(8,128)(2,1)} %all-gather.7.cloned.1.call-done) | copy-start | bytes 4718596
  539.9 0.7 copy-start.6
  616.6 15.0 %copy-start.5 = (bf16[256,256]{0,1:T(8,128)(2,1)S(1)}, bf16[256,256]{0,1:T(8,128)(2,1)}, u32[]{:S(2)}) copy-start(bf16[256,256]{0,1:T(8,128)(2,1)} %fusion.19) | copy-start | bytes 393220
Sparse Core Ops, SparseCore 0:
  45.2 44.4 all-gather.4
  93.5 64.4 reduce-scatter.1
  164.4 37.9 all-gather.6
  207.2 106.9 all-reduce.8
  316.4 104.4 all-gather.8
  433.3 103.7 all-reduce.10
  614.1 41.7 all-gather.10
where the time goes:
time: 700 us; the launch traced here: 699 us
  waiting for transfers between devices  466 us (67%)
  other arithmetic  73.8 us (11%)
  blocking collectives  71.5 us (10%)
  matrix products  39.3 us (6%)
  local copies, waits for them, and re-layouts  26.9 us (4%)
  between operations  15.8 us (2%)
    psum x1, waiting for transfers between devices, per_device(): lax.psum(grad_part.astype(jnp.bfloat16), 'dp').astype(jnp.float32)  107 us
    psum x1, waiting for transfers between devices, per_device(): gram_matrix = lax.psum(gram_local, 'fsdp')  103 us
    all_gather x1, waiting for transfers between devices, per_device(): lax.all_gather(right_prev, 'fsdp', axis=0, tiled=True)  94.7 us
    reduce_scatter x1, waiting for transfers between devices, per_device(): lax.psum_scatter(jnp.einsum('cd,ld->cl', weight_rows, cot_cols, preferred...  58.3 us
    all_gather x1, waiting for transfers between devices, per_device(): shard_piece = lax.all_gather(gated_out, 'fsdp', axis=1, tiled=True)  38 us
    another operation x7, other arithmetic, per_device(): lower_factor = jnp.linalg.cholesky(gram_matrix)  36.4 us
    psum x1, blocking collectives, per_device(): square_sums = lax.psum(jnp.sum(x_cols * x_cols, axis=1), 'fsdp')  34.9 us
    all_gather x1, waiting for transfers between devices, per_device(): lax.all_gather(normed_cols, 'fsdp', axis=1, tiled=True)  34.7 us
  transfers between devices with their start and end apart: 8, of which 8 were waited for; matrix products, arithmetic and copies ran while one was open for 6% of the time, Pallas kernels for 0%

commit v1 on v0

--- a/solution.py
+++ b/solution.py
@@ -109,7 +109,12 @@
         lax.psum(filter_part.astype(jnp.bfloat16), "dp").astype(jnp.float32),
     )
     grad_half = grad_total.astype(jnp.bfloat16)
-    grad_rows_own = lax.all_to_all(grad_half, "fsdp", split_axis=0, concat_axis=1, tiled=True)
+    grad_rows_own = jnp.concatenate(
+        lax.all_to_all(
+            jnp.stack(jnp.split(grad_half, lax.axis_size("fsdp"), axis=0)), "fsdp", 0, 0
+        ),
+        axis=1,
+    )
     panel_own = jnp.dot(
         grad_rows_own,
         lax.all_gather(right_prev, "fsdp", axis=0, tiled=True),

time: 700 us -> 729 us (1.041)
  local copies, waits for them, and re-layouts: 26.9 us -> 53.6 us
    all_to_all x1, waiting for transfers between devices: 6.47 us -> 102 us  [per_device(): lax.all_to_all(jnp.stack(jnp.split(grad_half, lax.axis_size('fsdp'), axis...]
    all_gather x1, waiting for transfers between devices: 94.7 us -> 0.01 us  [per_device(): lax.all_gather(right_prev, 'fsdp', axis=0, tiled=True)]
    unnamed x46 -> x61, local copies, waits for them, and re-layouts: 2.47 us -> 27.5 us
  transfers between devices with their start and end apart: 8 -> 8, of which waited for: 8 -> 7; matrix products, arithmetic and copies ran while one was open for 6% -> 5% of each run, Pallas kernels for 0% -> 0%
where the time goes in v1:
time: 729 us; the launch traced here: 727 us
  waiting for transfers between devices  467 us (64%)
  other arithmetic  73.8 us (10%)
  blocking collectives  71.5 us (10%)
  local copies, waits for them, and re-layouts  53.6 us (7%)
  matrix products  39.3 us (5%)
  between operations  15.8 us (2%)
    psum x1, waiting for transfers between devices, per_device(): lax.psum(grad_part.astype(jnp.bfloat16), 'dp').astype(jnp.float32)  107 us
    all_to_all x1, waiting for transfers between devices, per_device(): lax.all_to_all(jnp.stack(jnp.split(grad_half, lax.axis_size('fsdp'), axis...  102 us
    psum x1, waiting for transfers between devices, per_device(): gram_matrix = lax.psum(gram_local, 'fsdp')  102 us
    reduce_scatter x1, waiting for transfers between devices, per_device(): lax.psum_scatter(jnp.einsum('cd,ld->cl', weight_rows, cot_cols, preferred...  58.3 us
    all_gather x1, waiting for transfers between devices, per_device(): shard_piece = lax.all_gather(gated_out, 'fsdp', axis=1, tiled=True)  38 us
    another operation x7, other arithmetic, per_device(): lower_factor = jnp.linalg.cholesky(gram_matrix)  36.4 us
    psum x1, blocking collectives, per_device(): square_sums = lax.psum(jnp.sum(x_cols * x_cols, axis=1), 'fsdp')  34.9 us
    all_gather x1, waiting for transfers between devices, per_device(): lax.all_gather(normed_cols, 'fsdp', axis=1, tiled=True)  34.7 us
  transfers between devices with their start and end apart: 8, of which 7 were waited for; matrix products, arithmetic and copies ran while one was open for 5% of the time, Pallas kernels for 0%

profile of v1, /device:TPU:0, one launch (start us, length us, event | category | flops | bytes accessed | tf_op | source)
XLA Modules:
  0.0 727.0 jit_solution(6328092764293613914)
XLA Ops:
  9.3 34.9 %psum.35 = f32[192]{0:T(256)S(1)} all-reduce(f32[192]{0:T(256)S(1)} %get-tuple-element.121), channel_id=1, replica_groups=mesh['dp'=2,'fsdp'=16] {'fsdp'}, use_global_device_ids=true, to_apply=%region_1.0 | all-reduce | flops 192 | bytes 1536 | tf_op jit(solution)/shard_map/psum | solution.py:55
  45.1 5.4 fusion.30
  55.0 34.7 %all-gather.5.cloned.1.call-done = bf16[192,8192]{1,0:T(8,128)(2,1)} async-done(((bf16[192,512]{1,0:T(8,128)(2,1)}), bf16[192,8192]{1,0:T(8,128)(2,1)}) %all-gather.5.cloned.1.call-update) | async-done | bytes 3145744 | tf_op jit(solution)/shard_map/all_gather | solution.py:62
  89.7 9.8 %fusion.6 = bf16[3,192,256]{2,1,0:T(8,128)(2,1)S(1)} fusion(bf16[3,256,8192]{2,1,0:T(8,128)(2,1)} %param.12, bf16[192,8192]{1,0:T(8,128)(2,1)} %all-gather.5.cloned.1.call-done), kind=kOutput, calls=%fused_computation.8 | convolution fusion | flops 2416066560 | bytes 16023552 | tf_op jit(solution)/shard_map/ld,kcd->klc/dot_general | solution.py:60
  99.6 58.3 %reduce-scatter.2.cloned.1.call-done = f32[256,192]{0,1:T(8,128)} async-done(((f32[4096,192]{0,1:T(8,128)}), f32[256,192]{0,1:T(8,128)}) %reduce-scatter.2.cloned.1.call-update) | async-done | bytes 196624 | tf_op jit(solution)/shard_map/reduce_scatter | solution.py:83
  161.0 2.6 multiply_reduce_fusion.23
  164.3 38.0 %all-gather.7.cloned.1.call-done = bf16[192,4096]{1,0:T(8,128)(2,1)} async-done(((bf16[192,256]{1,0:T(8,128)(2,1)}), bf16[192,4096]{1,0:T(8,128)(2,1)}) %all-gather.7.cloned.1.call-update) | async-done | bytes 1572880 | tf_op jit(solution)/shard_map/all_gather | solution.py:76
  202.3 4.7 convolution_convert_fusion
  207.1 107.1 %all-reduce.9.cloned.1.call-done = bf16[4096,512]{1,0:T(8,128)(2,1)} async-done(((bf16[4096,512]{1,0:T(8,128)(2,1)}), bf16[4096,512]{1,0:T(8,128)(2,1)}) %all-reduce.9.cloned.1.call-update) | async-done | bytes 4194320 | tf_op jit(solution)/shard_map/psum | solution.py:108
  317.5 1.7 fusion.24
  329.2 1.7 fusion.17
  340.9 5.7 all-to-all-start
  347.2 102.3 %all-to-all-done = bf16[16,256,512]{2,1,0:T(8,128)(2,1)} async-done(((bf16[16,256,512]{2,1,0:T(8,128)(2,1)}), bf16[16,256,512]{2,1,0:T(8,128)(2,1)}, u32[]{:S(2)}, u32[]{:S(2)}) %all-to-all-start) | async-done | bytes 4194336 | tf_op jit(solution)/shard_map/all_to_all | solution.py:113
  449.6 6.4 copy.22
  455.9 4.8 convolution_convert_fusion.1
  462.5 102.1 %all-reduce.11.cloned.1.call-done = f32[256,256]{0,1:T(8,128)} async-done(((f32[256,256]{0,1:T(8,128)}), f32[256,256]{0,1:T(8,128)}) %all-reduce.11.cloned.1.call-update) | async-done | bytes 262160 | tf_op jit(solution)/shard_map/psum | solution.py:125
  564.7 1.8 copy.24
  568.2 11.7 %cholesky.50 = f32[128,128]{1,0:T(8,128)S(1)} custom-call(f32[128,128]{1,0:T(8,128)S(1)} %cholesky.118), custom_call_target="Cholesky" | custom-call | tf_op jit(solution)/shard_map/jit(cholesky)/cholesky | solution.py:126
  581.2 9.8 %custom-call.15 = f32[1,128,128]{1,2,0:T(8,128)S(1)} custom-call(f32[1,128,128]{2,1,0:T(8,128)S(1)} %get-tuple-element.89), custom_call_target="InvertDiagBlocksLowerTriangular" | custom-call | tf_op jit(solution)/shard_map/jit(cholesky)/cholesky | solution.py:126
  593.8 11.7 %cholesky.105 = f32[128,128]{1,0:T(8,128)S(1)} custom-call(f32[128,128]{1,0:T(8,128)S(1)} %convolution_subtract_fusion.1), custom_call_target="Cholesky" | custom-call | tf_op jit(solution)/shard_map/jit(cholesky)/cholesky | solution.py:126
  609.4 1.7 select_select_fusion
  611.8 6.8 while.1
  612.4 2.9 bitcast_dynamic-update-slice_fusion.2
  615.8 2.8 bitcast_dynamic-update-slice_fusion.2
  618.6 20.5 %custom-call.16 = f32[2,128,128]{1,2,0:T(8,128)S(1)} custom-call(f32[2,128,128]{2,1,0:T(8,128)} %get-tuple-element.11), custom_call_target="InvertDiagBlocksLowerTriangular" | custom-call | tf_op jit(solution)/shard_map/jit(_solve_triangular)/triangular_solve | solution.py:127
  641.7 1.9 multiply_reduce_fusion.2
  644.3 2.0 multiply_reduce_fusion.29
  649.8 5.0 psum.36
  655.4 3.8 fusion.9
  660.0 23.5 %all-gather.11.cloned.1.call-done = bf16[4096,256]{0,1:T(8,128)(2,1)} async-done(((bf16[256,256]{0,1:T(8,128)(2,1)}), bf16[4096,256]{0,1:T(8,128)(2,1)}) %all-gather.11.cloned.1.call-update) | async-done | bytes 2097168 | tf_op jit(solution)/shard_map/all_gather | solution.py:134
  683.5 4.2 multiply_reduce_fusion
  687.7 31.6 %psum.39 = f32[256]{0:T(256)S(1)} all-reduce(f32[256]{0:T(256)S(1)} %get-tuple-element.125), channel_id=1, replica_groups=mesh['dp'=2,'fsdp'=16] {'fsdp'}, use_global_device_ids=true, to_apply=%region_43.44 | all-reduce | flops 256 | bytes 2048 | tf_op jit(solution)/shard_map/psum | solution.py:137
  (206 shorter events, 56.1 us)
Async XLA Ops:
  7.2 1.1 copy-start
  7.2 82.5 %all-gather.5.cloned.1.call-start = ((), (), s32[]{:S(2)}) async-start(), calls=%async_computation.2 | async-start | bytes 3342336 | tf_op jit(solution)/shard_map/all_gather | solution.py:62
  45.0 5.5 copy-start.8
  45.0 6.6 copy-start.9
  45.1 112.9 %reduce-scatter.2.cloned.1.call-start = ((), (), s32[]{:S(2)}) async-start(), calls=%async_computation.4 | async-start | bytes 3342336 | tf_op jit(solution)/shard_map/reduce_scatter | solution.py:83
  50.5 151.8 %all-gather.7.cloned.1.call-start = ((), (), s32[]{:S(2)}) async-start(), calls=%async_computation.3 | async-start | bytes 1671168 | tf_op jit(solution)/shard_map/all_gather | solution.py:76
  99.5 102.8 %copy-start.7 = (bf16[1,192,512]{2,1,0:T(8,128)(2,1)S(1)}, bf16[1,192,512]{2,1,0:T(8,128)(2,1)}, u32[]{:S(2)}) copy-start(bf16[1,192,512]{2,1,0:T(8,128)(2,1)} %param.16) | copy-start | bytes 589828
  99.6 61.3 %copy-start.3 = (f32[192,256]{1,0:T(8,128)}, f32[192,256]{1,0:T(8,128)S(1)}, u32[]{:S(2)}) copy-start(f32[192,256]{1,0:T(8,128)S(1)} %get-tuple-element.84) | copy-start | bytes 589828
  159.1 48.0 %copy-start.4 = (f32[192,256]{1,0:T(8,128)}, f32[192,256]{1,0:T(8,128)S(1)}, u32[]{:S(2)}) copy-start(f32[192,256]{1,0:T(8,128)S(1)} %get-tuple-element.79) | copy-start | bytes 589828
  161.0 46.1 %copy-start.2 = (f32[192,256]{1,0:T(8,128)}, f32[192,256]{1,0:T(8,128)S(1)}, u32[]{:S(2)}) copy-start(f32[192,256]{1,0:T(8,128)S(1)} %mul.459) | copy-start | bytes 589828
  164.2 150.0 %all-reduce.9.cloned.1.call-start = ((), (), s32[]{:S(2)}) async-start(), calls=%async_computation.5 | async-start | bytes 8388608 | tf_op jit(solution)/shard_map/psum | solution.py:108
  340.9 108.6 %all-to-all-start = ((bf16[16,256,512]{2,1,0:T(8,128)(2,1)}), bf16[16,256,512]{2,1,0:T(8,128)(2,1)}, u32[]{:S(2)}, u32[]{:S(2)}) async-start(bf16[16,256,512]{2,1,0:T(8,128)(2,1)} %fusion.11), calls=%async_computation.1 | async-start | bytes 8388608 | tf_op jit(solution)/shard_map/all_to_all | solution.py:113
  346.6 109.3 %all-gather.9.cloned.1.call-start = ((), (), s32[]{:S(2)}) async-start(), calls=%async_computation.6 | async-start | bytes 4456448 | tf_op jit(solution)/shard_map/all_gather | solution.py:120
  347.2 217.5 %all-reduce.11.cloned.1.call-start = ((), (), s32[]{:S(2)}) async-start(), calls=%async_computation.7 | async-start | bytes 524288 | tf_op jit(solution)/shard_map/psum | solution.py:125
  461.7 221.9 %all-gather.11.cloned.1.call-start = ((), (), s32[]{:S(2)}) async-start(), calls=%async_computation.8 | async-start | bytes 2228224 | tf_op jit(solution)/shard_map/all_gather | solution.py:134
  462.5 192.9 %copy-start.1 = (bf16[192,4096]{1,0:T(8,128)(2,1)S(1)}, bf16[192,4096]{1,0:T(8,128)(2,1)}, u32[]{:S(2)}) copy-start(bf16[192,4096]{1,0:T(8,128)(2,1)} %all-gather.7.cloned.1.call-done) | copy-start | bytes 4718596
  567.5 0.7 copy-start.6
  644.2 15.0 %copy-start.5 = (bf16[256,256]{0,1:T(8,128)(2,1)S(1)}, bf16[256,256]{0,1:T(8,128)(2,1)}, u32[]{:S(2)}) copy-start(bf16[256,256]{0,1:T(8,128)(2,1)} %fusion.35) | copy-start | bytes 393220
Sparse Core Ops, SparseCore 0:
  45.2 44.4 all-gather.4
  93.5 64.4 reduce-scatter.1
  164.4 37.9 all-gather.6
  207.2 106.9 all-reduce.8
  349.5 94.3 all-gather.8
  461.8 102.8 all-reduce.10
  641.8 41.7 all-gather.10
